TPU v7x, 32 devices: a whole 2x2x4 slice. The times are simulated.
32 devices in a mesh: ctx: 8 (over z, y), head: 4 (over x, core).
Axes of the slice: x: 2, y: 2, z: 4, core: 2. Of those that a mesh axis runs over, the one named last changes fastest.
Arguments:
- queries: bfloat16 [2048, 6144], P(('ctx', 'head')), may hold values from -42 to 42
- key_head_columns: bfloat16 [2048, 512], P(('ctx', 'head')), may hold values from -4 to 4
- value_head_columns: bfloat16 [2048, 512], P(('ctx', 'head')), may hold values from -6 to 6
- output_gradient: bfloat16 [2048, 6144], P(('ctx', 'head')), may hold values from -6 to 6
- file_starts: int32 [5], replicated, may hold values from 0 to 1984, as said below
- file_imports: int32 [5, 4], replicated, may hold values from -1 to 4, as said below
- header_lens: int32 [5], replicated, may hold values from 16 to 64
Outputs:
- grad_queries: float32 [2048, 6144], P(('ctx', 'head'))
- key_gradient: float32 [2048, 512], P(('ctx', 'head'))
- value_gradient: float32 [2048, 512], P(('ctx', 'head'))
Inputs may be any that keep to these rules, and one draw needn't show every extreme that they name: `file_starts`: Increasing; the first is 0 and the last is 1984; each is a multiple of 64; no two lie in the same aligned block of 256 tokens; each file has 64 tokens or more. `file_imports`: each row lists distinct files other than its own, then -1 in the unused places; file 0 imports nothing.
All inputs are finite; a program needn't handle non-finite values.
Results may differ from a plain program's by a relative error of at most 0.004.
Values may be sent and summed in bfloat16 or wider, within the bound.
No kernel may reach another device: no remote copies, remote signals or barrier semaphores. Data moves between devices by JAX's collectives and lax.ppermute only.
A program may use at most 64 MiB of HBM per device.

v0:
```python
import math
import jax
import jax.numpy as jnp
from jax import lax
from jax.sharding import PartitionSpec as P

WIN = 1024
HDR = 64


def passed_along(value, axis, steps):
    count = lax.axis_size(axis)
    first, last = (max(0, -steps), min(count, count - steps))
    return lax.ppermute(value, axis, [(source, source + steps) for source in range(first, last)])


def local_files(file_starts, file_imports, header_lens, offset_base, span_rows):
    places = offset_base + jnp.arange(span_rows, dtype=jnp.int32)
    before = file_starts[None, :] <= places[:, None]
    file_of = jnp.sum(before.astype(jnp.int32), axis=1) - 1
    file_begin = jnp.max(jnp.where(before, file_starts[None, :], 0), axis=1)
    lower_file = file_of[0]
    upper_file = file_of[span_rows - 1]
    per_file = file_imports.shape[1]
    lower_list = lax.dynamic_slice_in_dim(file_imports, lower_file, 1, 0)[0]
    upper_list = lax.dynamic_slice_in_dim(file_imports, upper_file, 1, 0)[0]
    targets = jnp.concatenate([lower_list, upper_list])
    source_file = jnp.concatenate(
        [jnp.full((per_file,), lower_file, jnp.int32), jnp.full((per_file,), upper_file, jnp.int32)]
    )
    usable = (targets >= 0) & (
        (jnp.arange(2 * per_file, dtype=jnp.int32) < per_file) | (upper_file != lower_file)
    )
    matches = jnp.arange(file_starts.shape[0], dtype=jnp.int32)[None, :] == targets[:, None]
    target_start = jnp.sum(jnp.where(matches, file_starts[None, :], 0), axis=1)
    target_len = jnp.sum(jnp.where(matches, header_lens[None, :], 0), axis=1)
    return (places, file_of, file_begin, source_file, usable, target_start, target_len)


def visibility(places, file_of, file_begin, key_places, source_file, usable, target_len):
    window_ok = (
        (key_places[None, :] <= places[:, None])
        & (key_places[None, :] > places[:, None] - WIN)
        & (key_places[None, :] >= file_begin[:, None])
    )
    offsets = jnp.arange(usable.shape[0] * HDR, dtype=jnp.int32) % HDR
    header_ok = jnp.repeat(usable, HDR) & (offsets < jnp.repeat(target_len, HDR))
    header_vis = header_ok[None, :] & (file_of[:, None] == jnp.repeat(source_file, HDR)[None, :])
    return jnp.concatenate([window_ok, header_vis], axis=1)


def per_device(
    queries,
    key_head_columns,
    value_head_columns,
    output_gradient,
    file_starts,
    file_imports,
    header_lens,
):
    query_rows, key_rows, value_rows, grad_rows = (
        lax.all_to_all(queries, "head", split_axis=1, concat_axis=0, tiled=True),
        lax.all_to_all(key_head_columns, "head", split_axis=1, concat_axis=0, tiled=True),
        lax.all_to_all(value_head_columns, "head", split_axis=1, concat_axis=0, tiled=True),
        lax.all_to_all(output_gradient, "head", split_axis=1, concat_axis=0, tiled=True),
    )
    tokens_here = key_rows.shape[0]
    head_size = key_rows.shape[1]
    queries_per_group = query_rows.shape[1] // head_size
    shard_index = lax.axis_index("ctx")
    offset_base = shard_index * tokens_here
    scaling = 1.0 / math.sqrt(head_size)
    reach = WIN // tokens_here
    places, file_of, file_begin, source_file, usable, target_start, target_len = local_files(
        file_starts, file_imports, header_lens, offset_base, tokens_here
    )
    block_count = source_file.shape[0]
    stacked = jnp.concatenate([key_rows, value_rows], axis=1)
    earlier = []
    for distance in range(1, reach + 1):
        earlier.append(passed_along(stacked, "ctx", distance))
    inside = (file_starts >= offset_base) & (file_starts < offset_base + tokens_here)
    own_offset = jnp.sum(jnp.where(inside, file_starts - offset_base, 0))
    own_header = lax.dynamic_slice_in_dim(stacked, own_offset, HDR, 0)
    all_headers = lax.all_gather(own_header, "ctx", axis=0, tiled=True)
    header_rows = jnp.concatenate(
        [
            lax.dynamic_slice_in_dim(all_headers, target_start[index] // tokens_here * HDR, HDR, 0)
            for index in range(block_count)
        ],
        axis=0,
    )
    key_table = jnp.concatenate(earlier[::-1] + [stacked, header_rows], axis=0)
    key_matrix = key_table[:, :head_size]
    value_matrix = key_table[:, head_size:]
    window_len = (reach + 1) * tokens_here
    key_places = offset_base - reach * tokens_here + jnp.arange(window_len, dtype=jnp.int32)
    visible = visibility(places, file_of, file_begin, key_places, source_file, usable, target_len)
    heads_block = max(
        (
            divisor
            for divisor in range(1, queries_per_group + 1)
            if queries_per_group % divisor == 0 and divisor * tokens_here <= max(512, tokens_here)
        )
    )
    block_total = queries_per_group // heads_block
    query_blocks = (
        query_rows.reshape(tokens_here, queries_per_group, head_size)
        .transpose(1, 0, 2)
        .reshape(block_total, heads_block, tokens_here, head_size)
    )
    grad_blocks = (
        grad_rows.reshape(tokens_here, queries_per_group, head_size)
        .transpose(1, 0, 2)
        .reshape(block_total, heads_block, tokens_here, head_size)
    )

    def attend(carry, inputs):
        key_gradient_sum, value_gradient_sum = carry
        query_block, grad_block = inputs
        scores = (
            jnp.einsum("htd,kd->htk", query_block, key_matrix, preferred_element_type=jnp.float32)
            * scaling
        )
        scores = jnp.where(visible[None], scores, -jnp.inf)
        ceiling = jnp.max(scores, axis=-1, keepdims=True)
        log_total = ceiling + jnp.log(jnp.sum(jnp.exp(scores - ceiling), axis=-1, keepdims=True))
        weights = jnp.exp(scores - log_total)
        grad_weights = jnp.einsum(
            "htd,kd->htk", grad_block, value_matrix, preferred_element_type=jnp.float32
        )
        centre = jnp.sum(weights * grad_weights, axis=-1, keepdims=True)
        grad_scores = (weights * (grad_weights - centre)).astype(jnp.bfloat16)
        weights_low = weights.astype(jnp.bfloat16)
        grad_query = (
            jnp.einsum("htk,kd->htd", grad_scores, key_matrix, preferred_element_type=jnp.float32)
            * scaling
        )
        key_gradient_sum = (
            key_gradient_sum
            + jnp.einsum(
                "htk,htd->kd", grad_scores, query_block, preferred_element_type=jnp.float32
            )
            * scaling
        )
        value_gradient_sum = value_gradient_sum + jnp.einsum(
            "htk,htd->kd", weights_low, grad_block, preferred_element_type=jnp.float32
        )
        return ((key_gradient_sum, value_gradient_sum), grad_query)

    empty_gradient = jnp.zeros((key_table.shape[0], head_size), jnp.float32)
    (key_gradient_sum, value_gradient_sum), grad_query = lax.scan(
        attend, (empty_gradient, empty_gradient), (query_blocks, grad_blocks)
    )
    grad_query = (
        grad_query.reshape(queries_per_group, tokens_here, head_size)
        .transpose(1, 0, 2)
        .reshape(tokens_here, queries_per_group * head_size)
    )
    combined = jnp.concatenate([key_gradient_sum, value_gradient_sum], axis=1)

    def window_part(index):
        return combined[index * tokens_here : (index + 1) * tokens_here]

    collected = window_part(reach)
    for distance in range(1, reach + 1):
        collected = collected + passed_along(window_part(reach - distance), "ctx", -distance)
    header_part = combined[window_len:]
    blocks_out = header_part.reshape(block_count, HDR, 2 * head_size)
    holders = jnp.where(usable, target_start // tokens_here, -1)
    block_piece = lax.all_gather(blocks_out, "ctx", axis=0, tiled=True)
    holder_piece = lax.all_gather(holders, "ctx", axis=0, tiled=True)
    selected = (holder_piece == shard_index).astype(jnp.float32)
    arriving = jnp.einsum("m,mrc->rc", selected, block_piece)
    current = lax.dynamic_slice_in_dim(collected, own_offset, HDR, 0)
    collected = lax.dynamic_update_slice_in_dim(collected, current + arriving, own_offset, 0)
    grad_queries, key_gradient, value_gradient = (
        lax.all_to_all(grad_query, "head", split_axis=0, concat_axis=1, tiled=True),
        lax.all_to_all(collected[:, :head_size], "head", split_axis=0, concat_axis=1, tiled=True),
        lax.all_to_all(collected[:, head_size:], "head", split_axis=0, concat_axis=1, tiled=True),
    )
    return (grad_queries, key_gradient, value_gradient)


def solution(mesh):
    in_specs = (
        P(("ctx", "head"), None),
        P(("ctx", "head"), None),
        P(("ctx", "head"), None),
        P(("ctx", "head"), None),
        P(),
        P(),
        P(),
    )
    out_specs = (P(("ctx", "head"), None), P(("ctx", "head"), None), P(("ctx", "head"), None))
    return jax.shard_map(
        per_device, mesh=mesh, in_specs=in_specs, out_specs=out_specs, check_vma=False
    )
```

profile of v0, /device:TPU:0, one launch (start us, length us, event | category | flops | bytes accessed | tf_op | source)
XLA Modules:
  0.0 296.5 jit_solution(10358402667834652991)
XLA Ops:
  8.7 4.2 %all-to-all-start.1 = ((bf16[64,4,128]{2,0,1:T(8,128)(2,1)}), bf16[64,4,128]{2,0,1:T(8,128)(2,1)S(1)}, u32[]{:S(2)}, u32[]{:S(2)}) async-start(bf16[64,4,128]{2,0,1:T(8,128)(2,1)} %copy_bitcast_fusion.6), calls=%async_computation.1 | async-start | bytes 131072 | tf_op jit(solution)/shard_map/all_to_all | solution.py:63
  28.4 3.3 %all-to-all-start.2 = ((bf16[64,4,128]{2,0,1:T(8,128)(2,1)}), bf16[64,4,128]{2,0,1:T(8,128)(2,1)S(1)}, u32[]{:S(2)}, u32[]{:S(2)}) async-start(bf16[64,4,128]{2,0,1:T(8,128)(2,1)} %copy_bitcast_fusion.5), calls=%async_computation.2 | async-start | bytes 131072 | tf_op jit(solution)/shard_map/all_to_all | solution.py:64
  57.7 3.5 %all-to-all-start.3 = ((bf16[64,4,1536]{2,0,1:T(8,128)(2,1)}), bf16[64,4,1536]{2,0,1:T(8,128)(2,1)S(1)}, u32[]{:S(2)}, u32[]{:S(2)}) async-start(bf16[64,4,1536]{2,0,1:T(8,128)(2,1)} %bitcast.142), calls=%async_computation.3 | async-start | bytes 1572864 | tf_op jit(solution)/shard_map/all_to_all | solution.py:65
  61.2 5.0 %collective-permute-start = (bf16[256,256]{1,0:T(8,128)(2,1)S(1)}, bf16[256,256]{1,0:T(8,128)(2,1)S(1)}, u32[]{:S(2)}, u32[]{:S(2)}) collective-permute-start(bf16[256,256]{1,0:T(8,128)(2,1)S(1)} %pad_maximum_fusion), channel_id=1, source_target_pairs={{0,16},{4,20},{8,24},{12,28},{1,17},{5,21},{9,25},{13,29},{2,18},{... | collective-permute-start | bytes 393224 | tf_op jit(solution)/shard_map/ppermute | solution.py:14
  66.2 4.4 %collective-permute-start.1 = (bf16[256,256]{1,0:T(8,128)(2,1)S(1)}, bf16[256,256]{1,0:T(8,128)(2,1)S(1)}, u32[]{:S(2)}, u32[]{:S(2)}) collective-permute-start(bf16[256,256]{1,0:T(8,128)(2,1)S(1)} %pad_maximum_fusion), channel_id=1, source_target_pairs={{0,12},{4,16},{8,20},{12,24},{16,28},{1,13},{5,17},{9,21},{13,25},... | collective-permute-start | bytes 393224 | tf_op jit(solution)/shard_map/ppermute | solution.py:14
  72.0 3.1 %collective-permute-start.3 = (bf16[256,256]{1,0:T(8,128)(2,1)S(1)}, bf16[256,256]{1,0:T(8,128)(2,1)S(1)}, u32[]{:S(2)}, u32[]{:S(2)}) collective-permute-start(bf16[256,256]{1,0:T(8,128)(2,1)S(1)} %pad_maximum_fusion), channel_id=1, source_target_pairs={{0,4},{4,8},{8,12},{12,16},{16,20},{20,24},{24,28},{1,5},{5,9},{9,... | collective-permute-start | bytes 393224 | tf_op jit(solution)/shard_map/ppermute | solution.py:14
  75.1 31.9 %all_gather.9 = bf16[512,256]{1,0:T(8,128)(2,1)S(1)} all-gather(bf16[64,256]{1,0:T(8,128)(2,1)S(1)} %fusion.29), channel_id=1, replica_groups=mesh['ctx'=8,'head'=4] {'ctx'}, dimensions={0}, use_global_device_ids=true | all-gather | bytes 294912 | tf_op jit(solution)/shard_map/all_gather | solution.py:85
  114.7 4.2 %all-to-all-start = ((bf16[64,4,1536]{2,0,1:T(8,128)(2,1)}), bf16[64,4,1536]{2,0,1:T(8,128)(2,1)}, u32[]{:S(2)}, u32[]{:S(2)}) async-start(bf16[64,4,1536]{2,0,1:T(8,128)(2,1)} %bitcast.141), calls=%async_computation | async-start | bytes 1572864 | tf_op jit(solution)/shard_map/all_to_all | solution.py:62
  123.7 6.8 %all-to-all-done = bf16[64,4,1536]{2,0,1:T(8,128)(2,1)} async-done(((bf16[64,4,1536]{2,0,1:T(8,128)(2,1)}), bf16[64,4,1536]{2,0,1:T(8,128)(2,1)}, u32[]{:S(2)}, u32[]{:S(2)}) %all-to-all-start) | async-done | bytes 786464 | tf_op jit(solution)/shard_map/all_to_all | solution.py:62
  130.6 2.4 reshape.107
  133.0 2.3 copy.64
  135.3 68.0 %while.15 = (s32[]{:T(128)}, f32[1792,128]{1,0:T(8,128)S(1)}, f32[1792,128]{1,0:T(8,128)}, f32[6,2,256,128]{3,2,1,0:T(8,128)}, pred[256,1792]{1,0:T(8,128)(4,1)S...) while((s32[]{:T(128)}, f32[1792,128]{1,0:T(8,128)S(1)}, ...), condition=%wide.region_9.10_spmd.clone, body=%wide.region_5.9_spmd.clone.sunk | while | flops 1188461568 | bytes 80503144 | solution.py:152
  141.2 2.1 fusion.72
  143.4 2.9 fusion.73
  152.3 2.1 fusion.72
  154.4 3.3 %fusion.73 = f32[1792,128]{1,0:T(8,128)} fusion(f32[2,256,1792]{2,1,0:T(8,128)S(1)} %copy-done.2, f32[2,256]{1,0:T(2,128)S(1)} %log_add_fusion.2, f32[1792,128]{1,0:T(8,128)} %get-tuple-element.220, pred[]{:T(512)S(6)} %compare.23, bf16[6,2,256,128]{3,2,1,0:T(8,128)(2,1)} %copy-done.8, s32[]{:T(128)} %get-tuple-element.218), kind=kOutput, calls=%fused_computation.10.clone.1 | convolution fusion | flops 237174784 | bytes 5638657 | tf_op jit(solution)/shard_map/while/body/eval_jaxpr/htk,htd->kd/dot_general | solution.py:146
  163.7 2.1 fusion.72
  165.8 3.3 %fusion.73 = f32[1792,128]{1,0:T(8,128)} fusion(f32[2,256,1792]{2,1,0:T(8,128)S(1)} %copy-done.2, f32[2,256]{1,0:T(2,128)S(1)} %log_add_fusion.2, f32[1792,128]{1,0:T(8,128)} %get-tuple-element.220, pred[]{:T(512)S(6)} %compare.23, bf16[6,2,256,128]{3,2,1,0:T(8,128)(2,1)} %copy-done.8, s32[]{:T(128)} %get-tuple-element.218), kind=kOutput, calls=%fused_computation.10.clone.1 | convolution fusion | flops 237174784 | bytes 5638657 | tf_op jit(solution)/shard_map/while/body/eval_jaxpr/htk,htd->kd/dot_general | solution.py:146
  175.1 2.1 fusion.72
  177.2 3.3 %fusion.73 = f32[1792,128]{1,0:T(8,128)} fusion(f32[2,256,1792]{2,1,0:T(8,128)S(1)} %copy-done.2, f32[2,256]{1,0:T(2,128)S(1)} %log_add_fusion.2, f32[1792,128]{1,0:T(8,128)} %get-tuple-element.220, pred[]{:T(512)S(6)} %compare.23, bf16[6,2,256,128]{3,2,1,0:T(8,128)(2,1)} %copy-done.8, s32[]{:T(128)} %get-tuple-element.218), kind=kOutput, calls=%fused_computation.10.clone.1 | convolution fusion | flops 237174784 | bytes 5638657 | tf_op jit(solution)/shard_map/while/body/eval_jaxpr/htk,htd->kd/dot_general | solution.py:146
  186.5 2.1 fusion.72
  188.6 3.3 %fusion.73 = f32[1792,128]{1,0:T(8,128)} fusion(f32[2,256,1792]{2,1,0:T(8,128)S(1)} %copy-done.2, f32[2,256]{1,0:T(2,128)S(1)} %log_add_fusion.2, f32[1792,128]{1,0:T(8,128)} %get-tuple-element.220, pred[]{:T(512)S(6)} %compare.23, bf16[6,2,256,128]{3,2,1,0:T(8,128)(2,1)} %copy-done.8, s32[]{:T(128)} %get-tuple-element.218), kind=kOutput, calls=%fused_computation.10.clone.1 | convolution fusion | flops 237174784 | bytes 5638657 | tf_op jit(solution)/shard_map/while/body/eval_jaxpr/htk,htd->kd/dot_general | solution.py:146
  197.9 2.1 fusion.72
  200.0 3.3 %fusion.73 = f32[1792,128]{1,0:T(8,128)} fusion(f32[2,256,1792]{2,1,0:T(8,128)S(1)} %copy-done.2, f32[2,256]{1,0:T(2,128)S(1)} %log_add_fusion.2, f32[1792,128]{1,0:T(8,128)} %get-tuple-element.220, pred[]{:T(512)S(6)} %compare.23, bf16[6,2,256,128]{3,2,1,0:T(8,128)(2,1)} %copy-done.8, s32[]{:T(128)} %get-tuple-element.218), kind=kOutput, calls=%fused_computation.10.clone.1 | convolution fusion | flops 237174784 | bytes 5638657 | tf_op jit(solution)/shard_map/while/body/eval_jaxpr/htk,htd->kd/dot_general | solution.py:146
  211.8 2.4 copy.94
  215.5 3.6 %all-to-all-start.4 = ((f32[4,64,1536]{2,1,0:T(8,128)}), f32[4,64,1536]{2,1,0:T(8,128)S(1)}, u32[]{:S(2)}, u32[]{:S(2)}) async-start(f32[4,64,1536]{2,1,0:T(8,128)} %all_to_all.108), calls=%async_computation.4 | async-start | bytes 3145728 | tf_op jit(solution)/shard_map/all_to_all | solution.py:178
  219.1 48.7 %all-reduce.1 = s32[64]{0:T(128)S(1)} all-reduce(s32[64]{0:T(128)S(1)} %get-tuple-element.118), channel_id=1, replica_groups=mesh['ctx'=8,'head'=4] {'ctx'}, use_global_device_ids=true, to_apply=%add.1 | all-reduce | flops 64 | bytes 512
  269.1 2.8 fusion.24
  273.2 3.3 %all-to-all-start.6 = ((f32[4,64,128]{2,1,0:T(8,128)}), f32[4,64,128]{2,1,0:T(8,128)S(1)}, u32[]{:S(2)}, u32[]{:S(2)}) async-start(f32[4,64,128]{2,1,0:T(8,128)} %bitcast.29), calls=%async_computation.6 | async-start | bytes 262144 | tf_op jit(solution)/shard_map/all_to_all | solution.py:180
  277.8 3.3 %all-to-all-done.6 = f32[4,64,128]{2,1,0:T(8,128)S(1)} async-done(((f32[4,64,128]{2,1,0:T(8,128)}), f32[4,64,128]{2,1,0:T(8,128)S(1)}, u32[]{:S(2)}, u32[]{:S(2)}) %all-to-all-start.6) | async-done | bytes 131104 | tf_op jit(solution)/shard_map/all_to_all | solution.py:180
  281.1 3.3 %all-to-all-start.5 = ((f32[4,64,128]{2,1,0:T(8,128)}), f32[4,64,128]{2,1,0:T(8,128)S(1)}, u32[]{:S(2)}, u32[]{:S(2)}) async-start(f32[4,64,128]{2,1,0:T(8,128)} %bitcast.27), calls=%async_computation.5 | async-start | bytes 262144 | tf_op jit(solution)/shard_map/all_to_all | solution.py:179
  285.1 3.9 %all-to-all-done.5 = f32[4,64,128]{2,1,0:T(8,128)S(1)} async-done(((f32[4,64,128]{2,1,0:T(8,128)}), f32[4,64,128]{2,1,0:T(8,128)S(1)}, u32[]{:S(2)}, u32[]{:S(2)}) %all-to-all-start.5) | async-done | bytes 131104 | tf_op jit(solution)/shard_map/all_to_all | solution.py:179
  (224 shorter events, 78.5 us)
Async XLA Ops:
  7.2 47.8 %copy-start.11 = (bf16[64,6144]{1,0:T(8,128)(2,1)S(1)}, bf16[64,6144]{1,0:T(8,128)(2,1)}, u32[]{:S(2)}) copy-start(bf16[64,6144]{1,0:T(8,128)(2,1)} %param.12) | copy-start | bytes 2359300
  8.0 47.9 %copy-start.12 = (bf16[64,6144]{1,0:T(8,128)(2,1)S(1)}, bf16[64,6144]{1,0:T(8,128)(2,1)}, u32[]{:S(2)}) copy-start(bf16[64,6144]{1,0:T(8,128)(2,1)} %param.9) | copy-start | bytes 2359300
  8.7 19.7 %all-to-all-start.1 = ((bf16[64,4,128]{2,0,1:T(8,128)(2,1)}), bf16[64,4,128]{2,0,1:T(8,128)(2,1)S(1)}, u32[]{:S(2)}, u32[]{:S(2)}) async-start(bf16[64,4,128]{2,0,1:T(8,128)(2,1)} %copy_bitcast_fusion.6), calls=%async_computation.1 | async-start | bytes 131072 | tf_op jit(solution)/shard_map/all_to_all | solution.py:63
  28.4 29.3 %all-to-all-start.2 = ((bf16[64,4,128]{2,0,1:T(8,128)(2,1)}), bf16[64,4,128]{2,0,1:T(8,128)(2,1)S(1)}, u32[]{:S(2)}, u32[]{:S(2)}) async-start(bf16[64,4,128]{2,0,1:T(8,128)(2,1)} %copy_bitcast_fusion.5), calls=%async_computation.2 | async-start | bytes 131072 | tf_op jit(solution)/shard_map/all_to_all | solution.py:64
  57.7 57.0 %all-to-all-start.3 = ((bf16[64,4,1536]{2,0,1:T(8,128)(2,1)}), bf16[64,4,1536]{2,0,1:T(8,128)(2,1)S(1)}, u32[]{:S(2)}, u32[]{:S(2)}) async-start(bf16[64,4,1536]{2,0,1:T(8,128)(2,1)} %bitcast.142), calls=%async_computation.3 | async-start | bytes 1572864 | tf_op jit(solution)/shard_map/all_to_all | solution.py:65
  61.2 45.8 %collective-permute-start = (bf16[256,256]{1,0:T(8,128)(2,1)S(1)}, bf16[256,256]{1,0:T(8,128)(2,1)S(1)}, u32[]{:S(2)}, u32[]{:S(2)}) collective-permute-start(bf16[256,256]{1,0:T(8,128)(2,1)S(1)} %pad_maximum_fusion), channel_id=1, source_target_pairs={{0,16},{4,20},{8,24},{12,28},{1,17},{5,21},{9,25},{13,29},{2,18},{... | collective-permute-start | bytes 393224 | tf_op jit(solution)/shard_map/ppermute | solution.py:14
  66.2 41.5 %collective-permute-start.1 = (bf16[256,256]{1,0:T(8,128)(2,1)S(1)}, bf16[256,256]{1,0:T(8,128)(2,1)S(1)}, u32[]{:S(2)}, u32[]{:S(2)}) collective-permute-start(bf16[256,256]{1,0:T(8,128)(2,1)S(1)} %pad_maximum_fusion), channel_id=1, source_target_pairs={{0,12},{4,16},{8,20},{12,24},{16,28},{1,13},{5,17},{9,21},{13,25},... | collective-permute-start | bytes 393224 | tf_op jit(solution)/shard_map/ppermute | solution.py:14
  70.7 37.7 %collective-permute-start.2 = (bf16[256,256]{1,0:T(8,128)(2,1)S(1)}, bf16[256,256]{1,0:T(8,128)(2,1)S(1)}, u32[]{:S(2)}, u32[]{:S(2)}) collective-permute-start(bf16[256,256]{1,0:T(8,128)(2,1)S(1)} %pad_maximum_fusion), channel_id=1, source_target_pairs={{0,8},{4,12},{8,16},{12,20},{16,24},{20,28},{1,9},{5,13},{9,17},{1... | collective-permute-start | bytes 393224 | tf_op jit(solution)/shard_map/ppermute | solution.py:14
  72.0 37.0 %collective-permute-start.3 = (bf16[256,256]{1,0:T(8,128)(2,1)S(1)}, bf16[256,256]{1,0:T(8,128)(2,1)S(1)}, u32[]{:S(2)}, u32[]{:S(2)}) collective-permute-start(bf16[256,256]{1,0:T(8,128)(2,1)S(1)} %pad_maximum_fusion), channel_id=1, source_target_pairs={{0,4},{4,8},{8,12},{12,16},{16,20},{20,24},{24,28},{1,5},{5,9},{9,... | collective-permute-start | bytes 393224 | tf_op jit(solution)/shard_map/ppermute | solution.py:14
  114.7 15.9 %all-to-all-start = ((bf16[64,4,1536]{2,0,1:T(8,128)(2,1)}), bf16[64,4,1536]{2,0,1:T(8,128)(2,1)}, u32[]{:S(2)}, u32[]{:S(2)}) async-start(bf16[64,4,1536]{2,0,1:T(8,128)(2,1)} %bitcast.141), calls=%async_computation | async-start | bytes 1572864 | tf_op jit(solution)/shard_map/all_to_all | solution.py:62
  118.9 150.2 %all-gather.2.cloned.1.call-start = ((), (), s32[]{:S(2)}) async-start(), calls=%async_computation.7 | async-start | bytes 2359296 | tf_op jit(solution)/shard_map/all_gather | solution.py:171
  135.3 3.6 %copy-start.8 = (bf16[6,2,256,128]{3,2,1,0:T(8,128)(2,1)}, bf16[6,2,256,128]{3,2,1,0:T(8,128)(2,1)S(1)}, u32[]{:S(2)}) copy-start(bf16[6,2,256,128]{3,2,1,0:T(8,128)(2,1)S(1)} %get-tuple-element.236) | copy-start | bytes 2359300 | tf_op jit(solution)/shard_map/while
  146.3 3.6 %copy-start.8 = (bf16[6,2,256,128]{3,2,1,0:T(8,128)(2,1)}, bf16[6,2,256,128]{3,2,1,0:T(8,128)(2,1)S(1)}, u32[]{:S(2)}) copy-start(bf16[6,2,256,128]{3,2,1,0:T(8,128)(2,1)S(1)} %get-tuple-element.236) | copy-start | bytes 2359300 | tf_op jit(solution)/shard_map/while
  154.4 3.3 %copy-start.5 = (pred[256,1792]{1,0:T(8,128)(4,1)S(1)}, pred[256,1792]{1,0:T(8,128)(4,1)}, u32[]{:S(2)}) copy-start(pred[256,1792]{1,0:T(8,128)(4,1)} %copy-done.4) | copy-start | bytes 1376260 | tf_op jit(solution)/shard_map/while
  154.4 3.3 %copy-start.7 = (bf16[1792,128]{1,0:T(8,128)(2,1)S(1)}, bf16[1792,128]{1,0:T(8,128)(2,1)}, u32[]{:S(2)}) copy-start(bf16[1792,128]{1,0:T(8,128)(2,1)} %copy-done.6) | copy-start | bytes 1376260 | tf_op jit(solution)/shard_map/while
  157.7 3.6 %copy-start.8 = (bf16[6,2,256,128]{3,2,1,0:T(8,128)(2,1)}, bf16[6,2,256,128]{3,2,1,0:T(8,128)(2,1)S(1)}, u32[]{:S(2)}) copy-start(bf16[6,2,256,128]{3,2,1,0:T(8,128)(2,1)S(1)} %get-tuple-element.236) | copy-start | bytes 2359300 | tf_op jit(solution)/shard_map/while
  165.8 3.3 %copy-start.5 = (pred[256,1792]{1,0:T(8,128)(4,1)S(1)}, pred[256,1792]{1,0:T(8,128)(4,1)}, u32[]{:S(2)}) copy-start(pred[256,1792]{1,0:T(8,128)(4,1)} %copy-done.4) | copy-start | bytes 1376260 | tf_op jit(solution)/shard_map/while
  165.8 3.3 %copy-start.7 = (bf16[1792,128]{1,0:T(8,128)(2,1)S(1)}, bf16[1792,128]{1,0:T(8,128)(2,1)}, u32[]{:S(2)}) copy-start(bf16[1792,128]{1,0:T(8,128)(2,1)} %copy-done.6) | copy-start | bytes 1376260 | tf_op jit(solution)/shard_map/while
  169.1 3.6 %copy-start.8 = (bf16[6,2,256,128]{3,2,1,0:T(8,128)(2,1)}, bf16[6,2,256,128]{3,2,1,0:T(8,128)(2,1)S(1)}, u32[]{:S(2)}) copy-start(bf16[6,2,256,128]{3,2,1,0:T(8,128)(2,1)S(1)} %get-tuple-element.236) | copy-start | bytes 2359300 | tf_op jit(solution)/shard_map/while
  177.2 3.3 %copy-start.5 = (pred[256,1792]{1,0:T(8,128)(4,1)S(1)}, pred[256,1792]{1,0:T(8,128)(4,1)}, u32[]{:S(2)}) copy-start(pred[256,1792]{1,0:T(8,128)(4,1)} %copy-done.4) | copy-start | bytes 1376260 | tf_op jit(solution)/shard_map/while
  177.2 3.3 %copy-start.7 = (bf16[1792,128]{1,0:T(8,128)(2,1)S(1)}, bf16[1792,128]{1,0:T(8,128)(2,1)}, u32[]{:S(2)}) copy-start(bf16[1792,128]{1,0:T(8,128)(2,1)} %copy-done.6) | copy-start | bytes 1376260 | tf_op jit(solution)/shard_map/while
  180.5 3.6 %copy-start.8 = (bf16[6,2,256,128]{3,2,1,0:T(8,128)(2,1)}, bf16[6,2,256,128]{3,2,1,0:T(8,128)(2,1)S(1)}, u32[]{:S(2)}) copy-start(bf16[6,2,256,128]{3,2,1,0:T(8,128)(2,1)S(1)} %get-tuple-element.236) | copy-start | bytes 2359300 | tf_op jit(solution)/shard_map/while
  188.6 3.3 %copy-start.7 = (bf16[1792,128]{1,0:T(8,128)(2,1)S(1)}, bf16[1792,128]{1,0:T(8,128)(2,1)}, u32[]{:S(2)}) copy-start(bf16[1792,128]{1,0:T(8,128)(2,1)} %copy-done.6) | copy-start | bytes 1376260 | tf_op jit(solution)/shard_map/while
  191.9 3.6 %copy-start.8 = (bf16[6,2,256,128]{3,2,1,0:T(8,128)(2,1)}, bf16[6,2,256,128]{3,2,1,0:T(8,128)(2,1)S(1)}, u32[]{:S(2)}) copy-start(bf16[6,2,256,128]{3,2,1,0:T(8,128)(2,1)S(1)} %get-tuple-element.236) | copy-start | bytes 2359300 | tf_op jit(solution)/shard_map/while
  204.5 7.3 %copy-start.10 = (f32[1792,256]{1,0:T(8,128)}, f32[1792,256]{1,0:T(8,128)S(1)}, u32[]{:S(2)}) copy-start(f32[1792,256]{1,0:T(8,128)S(1)} %constant_dynamic-update-slice_fusion.13) | copy-start | bytes 5505028
  206.4 61.4 %collective-permute-start.4 = (f32[256,256]{1,0:T(8,128)}, f32[256,256]{1,0:T(8,128)S(1)}, u32[]{:S(2)}, u32[]{:S(2)}) collective-permute-start(f32[256,256]{1,0:T(8,128)} %get-tuple-element.124), channel_id=1, source_target_pairs={{4,0},{8,4},{12,8},{16,12},{20,16},{24,20},{28,24},{5,1},{9,5},{13... | collective-permute-start | bytes 786440 | tf_op jit(solution)/shard_map/ppermute | solution.py:14
  207.7 60.1 %collective-permute-start.5 = (f32[256,256]{1,0:T(8,128)}, f32[256,256]{1,0:T(8,128)S(1)}, u32[]{:S(2)}, u32[]{:S(2)}) collective-permute-start(f32[256,256]{1,0:T(8,128)} %get-tuple-element.127), channel_id=1, source_target_pairs={{8,0},{12,4},{16,8},{20,12},{24,16},{28,20},{9,1},{13,5},{17,9},{2... | collective-permute-start | bytes 786440 | tf_op jit(solution)/shard_map/ppermute | solution.py:14
  209.0 58.8 %collective-permute-start.6 = (f32[256,256]{1,0:T(8,128)}, f32[256,256]{1,0:T(8,128)}, u32[]{:S(2)}, u32[]{:S(2)}) collective-permute-start(f32[256,256]{1,0:T(8,128)} %get-tuple-element.126), channel_id=1, source_target_pairs={{12,0},{16,4},{20,8},{24,12},{28,16},{13,1},{17,5},{21,9},{25,13},... | collective-permute-start | bytes 786440 | tf_op jit(solution)/shard_map/ppermute | solution.py:14
  210.3 57.5 %collective-permute-start.7 = (f32[256,256]{1,0:T(8,128)}, f32[256,256]{1,0:T(8,128)}, u32[]{:S(2)}, u32[]{:S(2)}) collective-permute-start(f32[256,256]{1,0:T(8,128)} %get-tuple-element.125), channel_id=1, source_target_pairs={{16,0},{20,4},{24,8},{28,12},{17,1},{21,5},{25,9},{29,13},{18,2},{... | collective-permute-start | bytes 786440 | tf_op jit(solution)/shard_map/ppermute | solution.py:14
  215.5 57.6 %all-to-all-start.4 = ((f32[4,64,1536]{2,1,0:T(8,128)}), f32[4,64,1536]{2,1,0:T(8,128)S(1)}, u32[]{:S(2)}, u32[]{:S(2)}) async-start(f32[4,64,1536]{2,1,0:T(8,128)} %all_to_all.108), calls=%async_computation.4 | async-start | bytes 3145728 | tf_op jit(solution)/shard_map/all_to_all | solution.py:178
  273.2 7.9 %all-to-all-start.6 = ((f32[4,64,128]{2,1,0:T(8,128)}), f32[4,64,128]{2,1,0:T(8,128)S(1)}, u32[]{:S(2)}, u32[]{:S(2)}) async-start(f32[4,64,128]{2,1,0:T(8,128)} %bitcast.29), calls=%async_computation.6 | async-start | bytes 262144 | tf_op jit(solution)/shard_map/all_to_all | solution.py:180
  281.1 7.9 %all-to-all-start.5 = ((f32[4,64,128]{2,1,0:T(8,128)}), f32[4,64,128]{2,1,0:T(8,128)S(1)}, u32[]{:S(2)}, u32[]{:S(2)}) async-start(f32[4,64,128]{2,1,0:T(8,128)} %bitcast.27), calls=%async_computation.5 | async-start | bytes 262144 | tf_op jit(solution)/shard_map/all_to_all | solution.py:179
  (37 other events, 88.6 us)
Sparse Core Ops, SparseCore 0:
  205.5 60.7 all-gather.1
where the time goes:
time: 299 us; the launch traced here: 296 us
  blocking collectives  80.6 us (27%)
  matrix products  60.3 us (20%)
  starting transfers between devices  44.7 us (15%)
  between operations  43 us (14%)
  local copies, waits for them, and re-layouts  38.6 us (13%)
  other arithmetic  14.6 us (5%)
  waiting for transfers between devices  14.1 us (5%)
    unnamed x1, blocking collectives  48.7 us
    all_gather x1, blocking collectives, per_device(): all_headers = lax.all_gather(own_header, 'ctx', axis=0, tiled=True)  31.9 us
    dot_general x6, matrix products, attend(): jnp.einsum('htk,htd->kd', weights_low, grad_block, preferred_element_type...  19.3 us
    ppermute x8, starting transfers between devices, passed_along(): lax.ppermute(value, axis, [(source, source + steps) for source in range(f...  19.2 us
    dot_general x6, matrix products, attend(): jnp.einsum('htk,htd->kd', grad_scores, query_block, preferred_element_typ...  12.4 us
    dot_general x6, matrix products, attend(): jnp.einsum('htd,kd->htk', query_block, key_matrix, preferred_element_type...  11.8 us
    unnamed x24, local copies, waits for them, and re-layouts  10.3 us
    dot_general x6, matrix products, attend(): jnp.einsum('htk,kd->htd', grad_scores, key_matrix, preferred_element_type...  8.1 us
  transfers between devices with their start and end apart: 16, of which 3 were waited for; matrix products, arithmetic and copies ran while one was open for 12% of the time, Pallas kernels for 0%

commit v1 on v0

--- a/solution.py
+++ b/solution.py
@@ -82,7 +82,12 @@
     inside = (file_starts >= offset_base) & (file_starts < offset_base + tokens_here)
     own_offset = jnp.sum(jnp.where(inside, file_starts - offset_base, 0))
     own_header = lax.dynamic_slice_in_dim(stacked, own_offset, HDR, 0)
-    all_headers = lax.all_gather(own_header, "ctx", axis=0, tiled=True)
+    ring = [own_header]
+    for hop in range(7):
+        ring.append(lax.ppermute(ring[-1], "ctx", [(dev, (dev + 1) % 8) for dev in range(8)]))
+    all_headers = jnp.roll(
+        jnp.concatenate(ring[::-1], axis=0), (lax.axis_index("ctx") + 1) * ring[0].shape[0], axis=0
+    )
     header_rows = jnp.concatenate(
         [
             lax.dynamic_slice_in_dim(all_headers, target_start[index] // tokens_here * HDR, HDR, 0)

time: 299 us -> 300 us (level)
  blocking collectives: 80.6 us -> 38.5 us
  waiting for transfers between devices: 14.1 us -> 45.2 us
  starting transfers between devices: 44.7 us -> 53.5 us
  local copies, waits for them, and re-layouts: 38.6 us -> 41.8 us
    all_gather x1 -> x0, blocking collectives: 31.9 us -> none  [per_device(): all_headers = lax.all_gather(own_header, 'ctx', axis=0, tiled=True)]
    ppermute x0 -> x7, waiting for transfers between devices: none -> 26.2 us  [per_device(): lax.ppermute(ring[-1], 'ctx', [(dev, (dev + 1) % 8) for dev in range(8)])]
    unnamed x1, blocking collectives: 48.7 us -> 38.5 us
    all_gather x1, waiting for transfers between devices: 0.02 us -> 5.71 us  [per_device(): block_piece = lax.all_gather(blocks_out, 'ctx', axis=0, tiled=True)]
    ppermute x8, starting transfers between devices: 19.2 us -> 24.8 us  [passed_along(): lax.ppermute(value, axis, [(source, source + steps) for source in range(f...]
    ppermute x0 -> x7, starting transfers between devices: none -> 3.25 us  [per_device(): lax.ppermute(ring[-1], 'ctx', [(dev, (dev + 1) % 8) for dev in range(8)])]
    unnamed x24 -> x37, local copies, waits for them, and re-layouts: 10.3 us -> 10.5 us
  transfers between devices with their start and end apart: 16 -> 23, of which waited for: 3 -> 10; matrix products, arithmetic and copies ran while one was open for 12% -> 13% of each run, Pallas kernels for 0% -> 0%
where the time goes in v1:
time: 300 us; the launch traced here: 298 us
  matrix products  60.3 us (20%)
  starting transfers between devices  53.5 us (18%)
  waiting for transfers between devices  45.2 us (15%)
  between operations  43.2 us (14%)
  local copies, waits for them, and re-layouts  41.8 us (14%)
  blocking collectives  38.5 us (13%)
  other arithmetic  14.5 us (5%)
    unnamed x1, blocking collectives  38.5 us
    ppermute x7, waiting for transfers between devices, per_device(): lax.ppermute(ring[-1], 'ctx', [(dev, (dev + 1) % 8) for dev in range(8)])  26.2 us
    ppermute x8, starting transfers between devices, passed_along(): lax.ppermute(value, axis, [(source, source + steps) for source in range(f...  24.8 us
    dot_general x6, matrix products, attend(): jnp.einsum('htk,htd->kd', weights_low, grad_block, preferred_element_type...  19.2 us
    dot_general x6, matrix products, attend(): jnp.einsum('htk,htd->kd', grad_scores, query_block, preferred_element_typ...  12.5 us
    dot_general x6, matrix products, attend(): jnp.einsum('htd,kd->htk', query_block, key_matrix, preferred_element_type...  11.9 us
    unnamed x37, local copies, waits for them, and re-layouts  10.5 us
    dot_general x6, matrix products, attend(): jnp.einsum('htk,kd->htd', grad_scores, key_matrix, preferred_element_type...  8.1 us
  transfers between devices with their start and end apart: 23, of which 10 were waited for; matrix products, arithmetic and copies ran while one was open for 13% of the time, Pallas kernels for 0%

profile of v1, /device:TPU:0, one launch (start us, length us, event | category | flops | bytes accessed | tf_op | source)
XLA Modules:
  0.0 297.5 jit_solution(8920483604327314060)
XLA Ops:
  8.7 4.2 %all-to-all-start.1 = ((bf16[64,4,128]{2,0,1:T(8,128)(2,1)}), bf16[64,4,128]{2,0,1:T(8,128)(2,1)S(1)}, u32[]{:S(2)}, u32[]{:S(2)}) async-start(bf16[64,4,128]{2,0,1:T(8,128)(2,1)} %copy_bitcast_fusion.6), calls=%async_computation.1 | async-start | bytes 131072 | tf_op jit(solution)/shard_map/all_to_all | solution.py:63
  27.3 3.3 %all-to-all-start.2 = ((bf16[64,4,128]{2,0,1:T(8,128)(2,1)}), bf16[64,4,128]{2,0,1:T(8,128)(2,1)S(1)}, u32[]{:S(2)}, u32[]{:S(2)}) async-start(bf16[64,4,128]{2,0,1:T(8,128)(2,1)} %copy_bitcast_fusion.5), calls=%async_computation.2 | async-start | bytes 131072 | tf_op jit(solution)/shard_map/all_to_all | solution.py:64
  36.0 3.5 %all-to-all-start.3 = ((bf16[64,4,1536]{2,0,1:T(8,128)(2,1)}), bf16[64,4,1536]{2,0,1:T(8,128)(2,1)S(1)}, u32[]{:S(2)}, u32[]{:S(2)}) async-start(bf16[64,4,1536]{2,0,1:T(8,128)(2,1)} %bitcast.108), calls=%async_computation.3 | async-start | bytes 1572864 | tf_op jit(solution)/shard_map/all_to_all | solution.py:65
  41.7 4.5 %collective-permute-start = (bf16[256,256]{1,0:T(8,128)(2,1)S(1)}, bf16[256,256]{1,0:T(8,128)(2,1)S(1)}, u32[]{:S(2)}, u32[]{:S(2)}) collective-permute-start(bf16[256,256]{1,0:T(8,128)(2,1)S(1)} %pad_maximum_fusion), channel_id=1, source_target_pairs={{0,16},{4,20},{8,24},{12,28},{1,17},{5,21},{9,25},{13,29},{2,18},{... | collective-permute-start | bytes 393224 | tf_op jit(solution)/shard_map/ppermute | solution.py:14
  47.8 3.1 %collective-permute-start.1 = (bf16[256,256]{1,0:T(8,128)(2,1)S(1)}, bf16[256,256]{1,0:T(8,128)(2,1)S(1)}, u32[]{:S(2)}, u32[]{:S(2)}) collective-permute-start(bf16[256,256]{1,0:T(8,128)(2,1)S(1)} %pad_maximum_fusion), channel_id=1, source_target_pairs={{0,12},{4,16},{8,20},{12,24},{16,28},{1,13},{5,17},{9,21},{13,25},... | collective-permute-start | bytes 393224 | tf_op jit(solution)/shard_map/ppermute | solution.py:14
  50.9 2.4 collective-permute-done.5
  77.1 6.5 %collective-permute-start.2 = (bf16[256,256]{1,0:T(8,128)(2,1)S(1)}, bf16[256,256]{1,0:T(8,128)(2,1)S(1)}, u32[]{:S(2)}, u32[]{:S(2)}) collective-permute-start(bf16[256,256]{1,0:T(8,128)(2,1)S(1)} %pad_maximum_fusion), channel_id=1, source_target_pairs={{0,8},{4,12},{8,16},{12,20},{16,24},{20,28},{1,9},{5,13},{9,17},{1... | collective-permute-start | bytes 393224 | tf_op jit(solution)/shard_map/ppermute | solution.py:14
  83.7 5.3 %collective-permute-start.3 = (bf16[256,256]{1,0:T(8,128)(2,1)S(1)}, bf16[256,256]{1,0:T(8,128)(2,1)S(1)}, u32[]{:S(2)}, u32[]{:S(2)}) collective-permute-start(bf16[256,256]{1,0:T(8,128)(2,1)S(1)} %pad_maximum_fusion), channel_id=1, source_target_pairs={{0,4},{4,8},{8,12},{12,16},{16,20},{20,24},{24,28},{1,5},{5,9},{9,... | collective-permute-start | bytes 393224 | tf_op jit(solution)/shard_map/ppermute | solution.py:14
  90.4 5.3 %collective-permute-done.7 = bf16[64,256]{1,0:T(8,128)(2,1)S(1)} collective-permute-done((bf16[64,256]{1,0:T(8,128)(2,1)S(1)}, bf16[64,256]{1,0:T(8,128)(2,1)S(1)}, u32[]{:S(2)}, u32[]{:S(2)}) %collective-permute-start.7) | collective-permute-done | bytes 32800 | tf_op jit(solution)/shard_map/ppermute | solution.py:87
  96.3 5.9 %collective-permute-done.8 = bf16[64,256]{1,0:T(8,128)(2,1)S(1)} collective-permute-done((bf16[64,256]{1,0:T(8,128)(2,1)S(1)}, bf16[64,256]{1,0:T(8,128)(2,1)S(1)}, u32[]{:S(2)}, u32[]{:S(2)}) %collective-permute-start.8) | collective-permute-done | bytes 32800 | tf_op jit(solution)/shard_map/ppermute | solution.py:87
  102.9 6.1 %collective-permute-done.9 = bf16[64,256]{1,0:T(8,128)(2,1)S(1)} collective-permute-done((bf16[64,256]{1,0:T(8,128)(2,1)S(1)}, bf16[64,256]{1,0:T(8,128)(2,1)S(1)}, u32[]{:S(2)}, u32[]{:S(2)}) %collective-permute-start.9) | collective-permute-done | bytes 32800 | tf_op jit(solution)/shard_map/ppermute | solution.py:87
  109.7 5.9 %collective-permute-done.10 = bf16[64,256]{1,0:T(8,128)(2,1)S(1)} collective-permute-done((bf16[64,256]{1,0:T(8,128)(2,1)S(1)}, bf16[64,256]{1,0:T(8,128)(2,1)S(1)}, u32[]{:S(2)}, u32[]{:S(2)}) %collective-permute-start.10) | collective-permute-done | bytes 32800 | tf_op jit(solution)/shard_map/ppermute | solution.py:87
  120.4 4.2 %all-to-all-start = ((bf16[64,4,1536]{2,0,1:T(8,128)(2,1)}), bf16[64,4,1536]{2,0,1:T(8,128)(2,1)}, u32[]{:S(2)}, u32[]{:S(2)}) async-start(bf16[64,4,1536]{2,0,1:T(8,128)(2,1)} %bitcast.141), calls=%async_computation | async-start | bytes 1572864 | tf_op jit(solution)/shard_map/all_to_all | solution.py:62
  130.2 6.1 %all-to-all-done = bf16[64,4,1536]{2,0,1:T(8,128)(2,1)} async-done(((bf16[64,4,1536]{2,0,1:T(8,128)(2,1)}), bf16[64,4,1536]{2,0,1:T(8,128)(2,1)}, u32[]{:S(2)}, u32[]{:S(2)}) %all-to-all-start) | async-done | bytes 786464 | tf_op jit(solution)/shard_map/all_to_all | solution.py:62
  136.2 2.4 reshape.107
  138.6 2.3 copy.64
  141.0 68.0 %while.15 = (s32[]{:T(128)}, f32[1792,128]{1,0:T(8,128)S(1)}, f32[1792,128]{1,0:T(8,128)}, f32[6,2,256,128]{3,2,1,0:T(8,128)}, pred[256,1792]{1,0:T(8,128)(4,1)S...) while((s32[]{:T(128)}, f32[1792,128]{1,0:T(8,128)S(1)}, ...), condition=%wide.region_9.10_spmd.clone, body=%wide.region_5.9_spmd.clone.sunk | while | flops 1188461568 | bytes 80503144 | solution.py:157
  149.0 2.9 fusion.73
  160.1 3.3 %fusion.73 = f32[1792,128]{1,0:T(8,128)} fusion(f32[2,256,1792]{2,1,0:T(8,128)S(1)} %copy-done.2, f32[2,256]{1,0:T(2,128)S(1)} %log_add_fusion.2, f32[1792,128]{1,0:T(8,128)} %get-tuple-element.220, pred[]{:T(512)S(6)} %compare.24, bf16[6,2,256,128]{3,2,1,0:T(8,128)(2,1)} %copy-done.8, s32[]{:T(128)} %get-tuple-element.218), kind=kOutput, calls=%fused_computation.10.clone.1 | convolution fusion | flops 237174784 | bytes 5638657 | tf_op jit(solution)/shard_map/while/body/eval_jaxpr/htk,htd->kd/dot_general | solution.py:151
  171.5 3.3 %fusion.73 = f32[1792,128]{1,0:T(8,128)} fusion(f32[2,256,1792]{2,1,0:T(8,128)S(1)} %copy-done.2, f32[2,256]{1,0:T(2,128)S(1)} %log_add_fusion.2, f32[1792,128]{1,0:T(8,128)} %get-tuple-element.220, pred[]{:T(512)S(6)} %compare.24, bf16[6,2,256,128]{3,2,1,0:T(8,128)(2,1)} %copy-done.8, s32[]{:T(128)} %get-tuple-element.218), kind=kOutput, calls=%fused_computation.10.clone.1 | convolution fusion | flops 237174784 | bytes 5638657 | tf_op jit(solution)/shard_map/while/body/eval_jaxpr/htk,htd->kd/dot_general | solution.py:151
  182.9 3.3 %fusion.73 = f32[1792,128]{1,0:T(8,128)} fusion(f32[2,256,1792]{2,1,0:T(8,128)S(1)} %copy-done.2, f32[2,256]{1,0:T(2,128)S(1)} %log_add_fusion.2, f32[1792,128]{1,0:T(8,128)} %get-tuple-element.220, pred[]{:T(512)S(6)} %compare.24, bf16[6,2,256,128]{3,2,1,0:T(8,128)(2,1)} %copy-done.8, s32[]{:T(128)} %get-tuple-element.218), kind=kOutput, calls=%fused_computation.10.clone.1 | convolution fusion | flops 237174784 | bytes 5638657 | tf_op jit(solution)/shard_map/while/body/eval_jaxpr/htk,htd->kd/dot_general | solution.py:151
  194.3 3.3 %fusion.73 = f32[1792,128]{1,0:T(8,128)} fusion(f32[2,256,1792]{2,1,0:T(8,128)S(1)} %copy-done.2, f32[2,256]{1,0:T(2,128)S(1)} %log_add_fusion.2, f32[1792,128]{1,0:T(8,128)} %get-tuple-element.220, pred[]{:T(512)S(6)} %compare.24, bf16[6,2,256,128]{3,2,1,0:T(8,128)(2,1)} %copy-done.8, s32[]{:T(128)} %get-tuple-element.218), kind=kOutput, calls=%fused_computation.10.clone.1 | convolution fusion | flops 237174784 | bytes 5638657 | tf_op jit(solution)/shard_map/while/body/eval_jaxpr/htk,htd->kd/dot_general | solution.py:151
  205.6 3.3 %fusion.73 = f32[1792,128]{1,0:T(8,128)} fusion(f32[2,256,1792]{2,1,0:T(8,128)S(1)} %copy-done.2, f32[2,256]{1,0:T(2,128)S(1)} %log_add_fusion.2, f32[1792,128]{1,0:T(8,128)} %get-tuple-element.220, pred[]{:T(512)S(6)} %compare.24, bf16[6,2,256,128]{3,2,1,0:T(8,128)(2,1)} %copy-done.8, s32[]{:T(128)} %get-tuple-element.218), kind=kOutput, calls=%fused_computation.10.clone.1 | convolution fusion | flops 237174784 | bytes 5638657 | tf_op jit(solution)/shard_map/while/body/eval_jaxpr/htk,htd->kd/dot_general | solution.py:151
  217.4 2.4 copy.94
  221.1 3.6 %all-to-all-start.4 = ((f32[4,64,1536]{2,1,0:T(8,128)}), f32[4,64,1536]{2,1,0:T(8,128)S(1)}, u32[]{:S(2)}, u32[]{:S(2)}) async-start(f32[4,64,1536]{2,1,0:T(8,128)} %all_to_all.108), calls=%async_computation.4 | async-start | bytes 3145728 | tf_op jit(solution)/shard_map/all_to_all | solution.py:183
  224.7 38.5 %all-reduce.1 = s32[64]{0:T(128)S(1)} all-reduce(s32[64]{0:T(128)S(1)} %get-tuple-element.118), channel_id=1, replica_groups=mesh['ctx'=8,'head'=4] {'ctx'}, use_global_device_ids=true, to_apply=%add.1 | all-reduce | flops 64 | bytes 512
  264.4 5.7 %all-gather.2.cloned.1.call-done = bf16[64,64,256]{2,1,0:T(8,128)(2,1)} async-done(((bf16[8,64,256]{2,1,0:T(8,128)(2,1)}), bf16[64,64,256]{2,1,0:T(8,128)(2,1)}) %all-gather.2.cloned.1.call-update) | async-done | bytes 2097168 | tf_op jit(solution)/shard_map/all_gather | solution.py:176
  270.1 2.8 fusion.24
  274.2 3.3 %all-to-all-start.6 = ((f32[4,64,128]{2,1,0:T(8,128)}), f32[4,64,128]{2,1,0:T(8,128)S(1)}, u32[]{:S(2)}, u32[]{:S(2)}) async-start(f32[4,64,128]{2,1,0:T(8,128)} %bitcast.29), calls=%async_computation.6 | async-start | bytes 262144 | tf_op jit(solution)/shard_map/all_to_all | solution.py:185
  278.8 3.3 %all-to-all-done.6 = f32[4,64,128]{2,1,0:T(8,128)S(1)} async-done(((f32[4,64,128]{2,1,0:T(8,128)}), f32[4,64,128]{2,1,0:T(8,128)S(1)}, u32[]{:S(2)}, u32[]{:S(2)}) %all-to-all-start.6) | async-done | bytes 131104 | tf_op jit(solution)/shard_map/all_to_all | solution.py:185
  282.1 3.3 %all-to-all-start.5 = ((f32[4,64,128]{2,1,0:T(8,128)}), f32[4,64,128]{2,1,0:T(8,128)S(1)}, u32[]{:S(2)}, u32[]{:S(2)}) async-start(f32[4,64,128]{2,1,0:T(8,128)} %bitcast.27), calls=%async_computation.5 | async-start | bytes 262144 | tf_op jit(solution)/shard_map/all_to_all | solution.py:184
  286.1 3.9 %all-to-all-done.5 = f32[4,64,128]{2,1,0:T(8,128)S(1)} async-done(((f32[4,64,128]{2,1,0:T(8,128)}), f32[4,64,128]{2,1,0:T(8,128)S(1)}, u32[]{:S(2)}, u32[]{:S(2)}) %all-to-all-start.5) | async-done | bytes 131104 | tf_op jit(solution)/shard_map/all_to_all | solution.py:184
  (251 shorter events, 96.6 us)
Async XLA Ops:
  8.7 18.6 %all-to-all-start.1 = ((bf16[64,4,128]{2,0,1:T(8,128)(2,1)}), bf16[64,4,128]{2,0,1:T(8,128)(2,1)S(1)}, u32[]{:S(2)}, u32[]{:S(2)}) async-start(bf16[64,4,128]{2,0,1:T(8,128)(2,1)} %copy_bitcast_fusion.6), calls=%async_computation.1 | async-start | bytes 131072 | tf_op jit(solution)/shard_map/all_to_all | solution.py:63
  27.3 8.7 %all-to-all-start.2 = ((bf16[64,4,128]{2,0,1:T(8,128)(2,1)}), bf16[64,4,128]{2,0,1:T(8,128)(2,1)S(1)}, u32[]{:S(2)}, u32[]{:S(2)}) async-start(bf16[64,4,128]{2,0,1:T(8,128)(2,1)} %copy_bitcast_fusion.5), calls=%async_computation.2 | async-start | bytes 131072 | tf_op jit(solution)/shard_map/all_to_all | solution.py:64
  36.0 84.4 %all-to-all-start.3 = ((bf16[64,4,1536]{2,0,1:T(8,128)(2,1)}), bf16[64,4,1536]{2,0,1:T(8,128)(2,1)S(1)}, u32[]{:S(2)}, u32[]{:S(2)}) async-start(bf16[64,4,1536]{2,0,1:T(8,128)(2,1)} %bitcast.108), calls=%async_computation.3 | async-start | bytes 1572864 | tf_op jit(solution)/shard_map/all_to_all | solution.py:65
  39.5 7.2 %collective-permute-start.4 = (bf16[64,256]{1,0:T(8,128)(2,1)S(1)}, bf16[64,256]{1,0:T(8,128)(2,1)S(1)}, u32[]{:S(2)}, u32[]{:S(2)}) collective-permute-start(bf16[64,256]{1,0:T(8,128)(2,1)S(1)} %fusion.29), channel_id=1, source_target_pairs={{0,4},{4,8},{8,12},{12,16},{16,20},{20,24},{24,28},{28,0},{1,5},{5... | collective-permute-start | bytes 98312 | tf_op jit(solution)/shard_map/ppermute | solution.py:87
  41.7 47.4 %collective-permute-start = (bf16[256,256]{1,0:T(8,128)(2,1)S(1)}, bf16[256,256]{1,0:T(8,128)(2,1)S(1)}, u32[]{:S(2)}, u32[]{:S(2)}) collective-permute-start(bf16[256,256]{1,0:T(8,128)(2,1)S(1)} %pad_maximum_fusion), channel_id=1, source_target_pairs={{0,16},{4,20},{8,24},{12,28},{1,17},{5,21},{9,25},{13,29},{2,18},{... | collective-permute-start | bytes 393224 | tf_op jit(solution)/shard_map/ppermute | solution.py:14
  46.7 6.6 %collective-permute-start.5 = (bf16[64,256]{1,0:T(8,128)(2,1)S(1)}, bf16[64,256]{1,0:T(8,128)(2,1)S(1)}, u32[]{:S(2)}, u32[]{:S(2)}) collective-permute-start(bf16[64,256]{1,0:T(8,128)(2,1)S(1)} %collective-permute-done.4), channel_id=1, source_target_pairs={{0,4},{4,8},{8,12},{12,16},{16,20},{20,24},{24,28},{28,0},{1,5},{5... | collective-permute-start | bytes 98312 | tf_op jit(solution)/shard_map/ppermute | solution.py:87
  47.8 41.9 %collective-permute-start.1 = (bf16[256,256]{1,0:T(8,128)(2,1)S(1)}, bf16[256,256]{1,0:T(8,128)(2,1)S(1)}, u32[]{:S(2)}, u32[]{:S(2)}) collective-permute-start(bf16[256,256]{1,0:T(8,128)(2,1)S(1)} %pad_maximum_fusion), channel_id=1, source_target_pairs={{0,12},{4,16},{8,20},{12,24},{16,28},{1,13},{5,17},{9,21},{13,25},... | collective-permute-start | bytes 393224 | tf_op jit(solution)/shard_map/ppermute | solution.py:14
  53.3 35.7 %collective-permute-start.6 = (bf16[64,256]{1,0:T(8,128)(2,1)S(1)}, bf16[64,256]{1,0:T(8,128)(2,1)S(1)}, u32[]{:S(2)}, u32[]{:S(2)}) collective-permute-start(bf16[64,256]{1,0:T(8,128)(2,1)S(1)} %collective-permute-done.5), channel_id=1, source_target_pairs={{0,4},{4,8},{8,12},{12,16},{16,20},{20,24},{24,28},{28,0},{1,5},{5... | collective-permute-start | bytes 98312 | tf_op jit(solution)/shard_map/ppermute | solution.py:87
  77.1 18.5 %collective-permute-start.2 = (bf16[256,256]{1,0:T(8,128)(2,1)S(1)}, bf16[256,256]{1,0:T(8,128)(2,1)S(1)}, u32[]{:S(2)}, u32[]{:S(2)}) collective-permute-start(bf16[256,256]{1,0:T(8,128)(2,1)S(1)} %pad_maximum_fusion), channel_id=1, source_target_pairs={{0,8},{4,12},{8,16},{12,20},{16,24},{20,28},{1,9},{5,13},{9,17},{1... | collective-permute-start | bytes 393224 | tf_op jit(solution)/shard_map/ppermute | solution.py:14
  83.7 18.6 %collective-permute-start.3 = (bf16[256,256]{1,0:T(8,128)(2,1)S(1)}, bf16[256,256]{1,0:T(8,128)(2,1)S(1)}, u32[]{:S(2)}, u32[]{:S(2)}) collective-permute-start(bf16[256,256]{1,0:T(8,128)(2,1)S(1)} %pad_maximum_fusion), channel_id=1, source_target_pairs={{0,4},{4,8},{8,12},{12,16},{16,20},{20,24},{24,28},{1,5},{5,9},{9,... | collective-permute-start | bytes 393224 | tf_op jit(solution)/shard_map/ppermute | solution.py:14
  89.0 6.7 %collective-permute-start.7 = (bf16[64,256]{1,0:T(8,128)(2,1)S(1)}, bf16[64,256]{1,0:T(8,128)(2,1)S(1)}, u32[]{:S(2)}, u32[]{:S(2)}) collective-permute-start(bf16[64,256]{1,0:T(8,128)(2,1)S(1)} %collective-permute-done.6), channel_id=1, source_target_pairs={{0,4},{4,8},{8,12},{12,16},{16,20},{20,24},{24,28},{28,0},{1,5},{5... | collective-permute-start | bytes 98312 | tf_op jit(solution)/shard_map/ppermute | solution.py:87
  95.6 6.6 %collective-permute-start.8 = (bf16[64,256]{1,0:T(8,128)(2,1)S(1)}, bf16[64,256]{1,0:T(8,128)(2,1)S(1)}, u32[]{:S(2)}, u32[]{:S(2)}) collective-permute-start(bf16[64,256]{1,0:T(8,128)(2,1)S(1)} %collective-permute-done.7), channel_id=1, source_target_pairs={{0,4},{4,8},{8,12},{12,16},{16,20},{20,24},{24,28},{28,0},{1,5},{5... | collective-permute-start | bytes 98312 | tf_op jit(solution)/shard_map/ppermute | solution.py:87
  102.3 6.8 %collective-permute-start.9 = (bf16[64,256]{1,0:T(8,128)(2,1)S(1)}, bf16[64,256]{1,0:T(8,128)(2,1)S(1)}, u32[]{:S(2)}, u32[]{:S(2)}) collective-permute-start(bf16[64,256]{1,0:T(8,128)(2,1)S(1)} %collective-permute-done.8), channel_id=1, source_target_pairs={{0,4},{4,8},{8,12},{12,16},{16,20},{20,24},{24,28},{28,0},{1,5},{5... | collective-permute-start | bytes 98312 | tf_op jit(solution)/shard_map/ppermute | solution.py:87
  109.1 6.6 %collective-permute-start.10 = (bf16[64,256]{1,0:T(8,128)(2,1)S(1)}, bf16[64,256]{1,0:T(8,128)(2,1)S(1)}, u32[]{:S(2)}, u32[]{:S(2)}) collective-permute-start(bf16[64,256]{1,0:T(8,128)(2,1)S(1)} %collective-permute-done.9), channel_id=1, source_target_pairs={{0,4},{4,8},{8,12},{12,16},{16,20},{20,24},{24,28},{28,0},{1,5},{5... | collective-permute-start | bytes 98312 | tf_op jit(solution)/shard_map/ppermute | solution.py:87
  115.9 3.9 %copy-start.11 = (bf16[1024,256]{1,0:T(8,128)(2,1)}, bf16[1024,256]{1,0:T(8,128)(2,1)S(1)}, u32[]{:S(2)}) copy-start(bf16[1024,256]{1,0:T(8,128)(2,1)S(1)} %constant_dynamic-update-slice_fusion) | copy-start | bytes 1572868
  120.4 15.9 %all-to-all-start = ((bf16[64,4,1536]{2,0,1:T(8,128)(2,1)}), bf16[64,4,1536]{2,0,1:T(8,128)(2,1)}, u32[]{:S(2)}, u32[]{:S(2)}) async-start(bf16[64,4,1536]{2,0,1:T(8,128)(2,1)} %bitcast.141), calls=%async_computation | async-start | bytes 1572864 | tf_op jit(solution)/shard_map/all_to_all | solution.py:62
  124.6 145.6 %all-gather.2.cloned.1.call-start = ((), (), s32[]{:S(2)}) async-start(), calls=%async_computation.7 | async-start | bytes 2359296 | tf_op jit(solution)/shard_map/all_gather | solution.py:176
  141.0 3.6 %copy-start.8 = (bf16[6,2,256,128]{3,2,1,0:T(8,128)(2,1)}, bf16[6,2,256,128]{3,2,1,0:T(8,128)(2,1)S(1)}, u32[]{:S(2)}) copy-start(bf16[6,2,256,128]{3,2,1,0:T(8,128)(2,1)S(1)} %get-tuple-element.236) | copy-start | bytes 2359300 | tf_op jit(solution)/shard_map/while
  152.0 3.6 %copy-start.8 = (bf16[6,2,256,128]{3,2,1,0:T(8,128)(2,1)}, bf16[6,2,256,128]{3,2,1,0:T(8,128)(2,1)S(1)}, u32[]{:S(2)}) copy-start(bf16[6,2,256,128]{3,2,1,0:T(8,128)(2,1)S(1)} %get-tuple-element.236) | copy-start | bytes 2359300 | tf_op jit(solution)/shard_map/while
  160.0 3.3 %copy-start.5 = (pred[256,1792]{1,0:T(8,128)(4,1)S(1)}, pred[256,1792]{1,0:T(8,128)(4,1)}, u32[]{:S(2)}) copy-start(pred[256,1792]{1,0:T(8,128)(4,1)} %copy-done.4) | copy-start | bytes 1376260 | tf_op jit(solution)/shard_map/while
  163.4 3.6 %copy-start.8 = (bf16[6,2,256,128]{3,2,1,0:T(8,128)(2,1)}, bf16[6,2,256,128]{3,2,1,0:T(8,128)(2,1)S(1)}, u32[]{:S(2)}) copy-start(bf16[6,2,256,128]{3,2,1,0:T(8,128)(2,1)S(1)} %get-tuple-element.236) | copy-start | bytes 2359300 | tf_op jit(solution)/shard_map/while
  174.8 3.6 %copy-start.8 = (bf16[6,2,256,128]{3,2,1,0:T(8,128)(2,1)}, bf16[6,2,256,128]{3,2,1,0:T(8,128)(2,1)S(1)}, u32[]{:S(2)}) copy-start(bf16[6,2,256,128]{3,2,1,0:T(8,128)(2,1)S(1)} %get-tuple-element.236) | copy-start | bytes 2359300 | tf_op jit(solution)/shard_map/while
  186.2 3.6 %copy-start.8 = (bf16[6,2,256,128]{3,2,1,0:T(8,128)(2,1)}, bf16[6,2,256,128]{3,2,1,0:T(8,128)(2,1)S(1)}, u32[]{:S(2)}) copy-start(bf16[6,2,256,128]{3,2,1,0:T(8,128)(2,1)S(1)} %get-tuple-element.236) | copy-start | bytes 2359300 | tf_op jit(solution)/shard_map/while
  197.6 3.6 %copy-start.8 = (bf16[6,2,256,128]{3,2,1,0:T(8,128)(2,1)}, bf16[6,2,256,128]{3,2,1,0:T(8,128)(2,1)S(1)}, u32[]{:S(2)}) copy-start(bf16[6,2,256,128]{3,2,1,0:T(8,128)(2,1)S(1)} %get-tuple-element.236) | copy-start | bytes 2359300 | tf_op jit(solution)/shard_map/while
  210.2 7.2 %copy-start.10 = (f32[1792,256]{1,0:T(8,128)}, f32[1792,256]{1,0:T(8,128)S(1)}, u32[]{:S(2)}) copy-start(f32[1792,256]{1,0:T(8,128)S(1)} %constant_dynamic-update-slice_fusion.29) | copy-start | bytes 5505028
  212.0 51.2 %collective-permute-start.11 = (f32[256,256]{1,0:T(8,128)}, f32[256,256]{1,0:T(8,128)S(1)}, u32[]{:S(2)}, u32[]{:S(2)}) collective-permute-start(f32[256,256]{1,0:T(8,128)} %get-tuple-element.124), channel_id=1, source_target_pairs={{4,0},{8,4},{12,8},{16,12},{20,16},{24,20},{28,24},{5,1},{9,5},{13... | collective-permute-start | bytes 786440 | tf_op jit(solution)/shard_map/ppermute | solution.py:14
  213.3 49.9 %collective-permute-start.12 = (f32[256,256]{1,0:T(8,128)}, f32[256,256]{1,0:T(8,128)S(1)}, u32[]{:S(2)}, u32[]{:S(2)}) collective-permute-start(f32[256,256]{1,0:T(8,128)} %get-tuple-element.127), channel_id=1, source_target_pairs={{8,0},{12,4},{16,8},{20,12},{24,16},{28,20},{9,1},{13,5},{17,9},{2... | collective-permute-start | bytes 786440 | tf_op jit(solution)/shard_map/ppermute | solution.py:14
  214.6 48.6 %collective-permute-start.13 = (f32[256,256]{1,0:T(8,128)}, f32[256,256]{1,0:T(8,128)}, u32[]{:S(2)}, u32[]{:S(2)}) collective-permute-start(f32[256,256]{1,0:T(8,128)} %get-tuple-element.126), channel_id=1, source_target_pairs={{12,0},{16,4},{20,8},{24,12},{28,16},{13,1},{17,5},{21,9},{25,13},... | collective-permute-start | bytes 786440 | tf_op jit(solution)/shard_map/ppermute | solution.py:14
  215.9 47.3 %collective-permute-start.14 = (f32[256,256]{1,0:T(8,128)}, f32[256,256]{1,0:T(8,128)}, u32[]{:S(2)}, u32[]{:S(2)}) collective-permute-start(f32[256,256]{1,0:T(8,128)} %get-tuple-element.125), channel_id=1, source_target_pairs={{16,0},{20,4},{24,8},{28,12},{17,1},{21,5},{25,9},{29,13},{18,2},{... | collective-permute-start | bytes 786440 | tf_op jit(solution)/shard_map/ppermute | solution.py:14
  221.1 53.1 %all-to-all-start.4 = ((f32[4,64,1536]{2,1,0:T(8,128)}), f32[4,64,1536]{2,1,0:T(8,128)S(1)}, u32[]{:S(2)}, u32[]{:S(2)}) async-start(f32[4,64,1536]{2,1,0:T(8,128)} %all_to_all.108), calls=%async_computation.4 | async-start | bytes 3145728 | tf_op jit(solution)/shard_map/all_to_all | solution.py:183
  274.2 7.9 %all-to-all-start.6 = ((f32[4,64,128]{2,1,0:T(8,128)}), f32[4,64,128]{2,1,0:T(8,128)S(1)}, u32[]{:S(2)}, u32[]{:S(2)}) async-start(f32[4,64,128]{2,1,0:T(8,128)} %bitcast.29), calls=%async_computation.6 | async-start | bytes 262144 | tf_op jit(solution)/shard_map/all_to_all | solution.py:185
  282.1 7.9 %all-to-all-start.5 = ((f32[4,64,128]{2,1,0:T(8,128)}), f32[4,64,128]{2,1,0:T(8,128)S(1)}, u32[]{:S(2)}, u32[]{:S(2)}) async-start(f32[4,64,128]{2,1,0:T(8,128)} %bitcast.27), calls=%async_computation.5 | async-start | bytes 262144 | tf_op jit(solution)/shard_map/all_to_all | solution.py:184
  (43 other events, 108.3 us)
Sparse Core Ops, SparseCore 0:
  211.1 58.9 all-gather.1
